TPU v7x, 128 devices: a whole 4x4x4 slice. The times are simulated.
128 devices in a mesh: rep: 4 (over z), ep: 32 (over y, x, core).
Axes of the slice: x: 4, y: 4, z: 4, core: 2. Of those that a mesh axis runs over, the one named last changes fastest.
Arguments:
- tokens: bfloat16 [16384, 2048], P(('rep', 'ep')), may hold values from -6 to 6
- experts: int32 [16384, 10], P(('rep', 'ep')), may hold values from 0 to 127, all different within a row; in each aligned block of 128 rows (0 to 127, 128 to 255, ...) at most 16 rows name the same one
- gates: bfloat16 [16384, 10], P(('rep', 'ep')), may hold values from 0.099609375 to 0.5
- w_gate: bfloat16 [128, 2048, 512], P('ep'), may hold values from -0.125 to 0.125
- w_up: bfloat16 [128, 2048, 512], P('ep'), may hold values from -0.125 to 0.125
- w_down: bfloat16 [128, 2048, 512], P('ep'), may hold values from -0.25 to 0.25
Outputs:
- mixed: bfloat16 [16384, 2048], P(('rep', 'ep'))
Inputs may be any that keep to these rules, and one draw needn't show every extreme that they name: Each row names 10 different experts. Among the 128 tokens of one device (aligned blocks of rows), no expert is named more than 16 times; in some such blocks one expert is named exactly 16 times.
All inputs are finite; a program needn't handle non-finite values.
Results may differ from a plain program's by a relative error of at most 0.0057.
Values may be sent and summed in bfloat16 or wider, within the bound.
A program may use at most 128 MiB of HBM per device.

v0:
```python
import jax
import jax.numpy as jnp
from jax import lax
from jax.sharding import PartitionSpec as P


def run_experts(rows, gate_w, up_w, down_w):
    gate_act = jnp.einsum("erd,edf->erf", rows, gate_w, preferred_element_type=jnp.float32)
    up_act = jnp.einsum("erd,edf->erf", rows, up_w, preferred_element_type=jnp.float32)
    hidden = (jax.nn.silu(gate_act) * up_act).astype(jnp.bfloat16)
    return jnp.einsum("erf,edf->erd", hidden, down_w, preferred_element_type=jnp.float32).astype(
        jnp.bfloat16
    )


def body(tokens, experts, gates, w_gate, w_up, w_down):
    n_ep = lax.axis_size("ep")
    tok_dev, width = tokens.shape
    topk = experts.shape[1]
    held = w_gate.shape[0]
    n_experts = held * n_ep
    capacity = 8 * tok_dev * topk // (5 * n_experts)
    slots = n_experts * capacity
    flat = experts.reshape(-1)
    onehot = (flat[:, None] == jnp.arange(n_experts, dtype=jnp.int32)[None, :]).astype(jnp.int32)
    position = jnp.sum(jnp.cumsum(onehot, axis=0) * onehot, axis=1) - 1
    target = (flat * capacity + position).reshape(tok_dev, topk)
    slot_ids = jnp.arange(slots, dtype=jnp.int32)
    matches = slot_ids[:, None, None] == target[None, :, :]
    spread = jnp.any(matches, axis=-1).astype(jnp.bfloat16)
    outgoing = jnp.dot(spread, tokens, preferred_element_type=jnp.float32).astype(jnp.bfloat16)
    by_owner = outgoing.reshape(n_ep, held, capacity, width)
    arrived = lax.all_to_all(by_owner, "ep", split_axis=0, concat_axis=2, tiled=True)
    results = run_experts(arrived[0], w_gate, w_up, w_down)
    returned = lax.all_to_all(results[None], "ep", split_axis=2, concat_axis=0, tiled=True)
    returned = returned.reshape(slots, width)
    weighting = jnp.sum(jnp.where(matches, gates.astype(jnp.float32)[None, :, :], 0.0), axis=-1)
    weighting = weighting.T.astype(jnp.bfloat16)
    mixed = jnp.dot(weighting, returned, preferred_element_type=jnp.float32)
    return mixed.astype(jnp.bfloat16)


def solution(mesh):
    in_specs = (
        P(("rep", "ep"), None),
        P(("rep", "ep"), None),
        P(("rep", "ep"), None),
        P("ep", None, None),
        P("ep", None, None),
        P("ep", None, None),
    )
    out_specs = P(("rep", "ep"), None)
    return jax.shard_map(body, mesh=mesh, in_specs=in_specs, out_specs=out_specs, check_vma=False)
```

profile of v0, /device:TPU:1, one launch (start us, length us, event | category | flops | bytes accessed | tf_op | source)
XLA Modules:
  0.0 290.5 jit_solution(10426558837764256989)
XLA Ops:
  0.0 0.9 copy.50
  0.9 0.1 eq.43
  1.0 0.1 eq.39
  1.1 0.1 copy.52
  1.2 0.3 fusion.2
  1.6 0.1 broadcast_add_fusion
  1.7 0.2 copy.53
  1.9 0.4 fusion.4
  2.4 0.1 sub.7
  2.5 0.1 copy.54
  2.6 0.7 multiply_add_fusion
  3.3 1.8 fusion
  5.1 2.3 convolution_convert_fusion
  7.5 104.2 %all_to_all.30 = bf16[32,4,16,2048]{3,2,1,0:T(8,128)(2,1)} all-to-all(bf16[32,4,16,2048]{3,2,1,0:T(8,128)(2,1)S(1)} %bitcast.30), channel_id=1, replica_groups=mesh['rep'=4,'ep'=32] {'ep'}, dimensions={0} | all-to-all | bytes 16777216 | tf_op jit(solution)/shard_map/all_to_all | solution.py:33
  111.6 8.3 %copy.55 = bf16[1,4,32,16,2048]{4,3,2,1,0:T(8,128)(2,1)} copy(bf16[1,4,32,16,2048]{4,3,1,2,0:T(8,128)(2,1)} %bitcast.31) | data formatting | bytes 16777216 | tf_op jit(solution)/shard_map/all_to_all | solution.py:33
  119.9 12.2 %fusion.8 = f32[4,512,512]{2,1,0:T(8,128)} fusion(bf16[4,512,2048]{2,1,0:T(8,128)(2,1)} %bitcast.33, bf16[4,2048,512]{2,1,0:T(8,128)(2,1)} %param.9), kind=kOutput, calls=%fused_computation.21 | convolution fusion | flops 4294967296 | bytes 20971520 | tf_op jit(solution)/shard_map/erd,edf->erf/dot_general | solution.py:8
  132.1 16.4 %convert_bitcast_fusion = bf16[1,4,512,2048]{3,2,1,0:T(8,128)(2,1)} fusion(bf16[4,2048,512]{2,1,0:T(8,128)(2,1)} %param.11, f32[4,512,512]{2,1,0:T(8,128)} %fusion.8, bf16[4,512,2048]{2,1,0:T(8,128)(2,1)} %bitcast.34, bf16[4,2048,512]{2,1,0:T(8,128)(2,1)} %param.10), kind=kOutput, calls=%fused_computation.3 | convolution fusion | flops 8600420352 | bytes 37748736 | tf_op jit(solution)/shard_map/erf,edf->erd/dot_general | solution.py:11
  148.4 12.1 %copy.56 = bf16[1,4,512,2048]{3,1,0,2:T(4,128)(2,1)} copy(bf16[1,4,512,2048]{3,2,1,0:T(8,128)(2,1)} %convert_bitcast_fusion) | data formatting | bytes 16777216 | tf_op jit(solution)/shard_map/broadcast_in_dim | solution.py:35
  160.6 5.1 %all-to-all-start.1 = ((bf16[1,4,512,2048]{3,1,0,2:T(4,128)(2,1)}), bf16[1,4,512,2048]{3,1,0,2:T(4,128)(2,1)}, u32[]{:S(2)}, u32[]{:S(2)}) async-start(bf16[1,4,512,2048]{3,1,0,2:T(4,128)(2,1)} %copy.56), calls=%async_computation.1 | async-start | bytes 16777216 | tf_op jit(solution)/shard_map/all_to_all | solution.py:35
  165.7 1.1 select_reduce_fusion
  166.8 98.7 %all-to-all-done.1 = bf16[1,4,512,2048]{3,1,0,2:T(4,128)(2,1)} async-done(((bf16[1,4,512,2048]{3,1,0,2:T(4,128)(2,1)}), bf16[1,4,512,2048]{3,1,0,2:T(4,128)(2,1)}, u32[]{:S(2)}, u32[]{:S(2)}) %all-to-all-start.1) | async-done | bytes 8388640 | tf_op jit(solution)/shard_map/all_to_all | solution.py:35
  265.5 11.2 %copy.57 = bf16[1,4,512,2048]{3,2,1,0:T(8,128)(2,1)} copy(bf16[1,4,512,2048]{3,1,0,2:T(4,128)(2,1)} %all-to-all-done.1) | data formatting | bytes 16777216 | tf_op jit(solution)/shard_map/all_to_all | solution.py:35
  276.7 8.3 %copy.58 = bf16[32,1,4,16,2048]{4,3,2,0,1:T(8,128)(2,1)} copy(bf16[32,1,4,16,2048]{4,3,0,2,1:T(8,128)(2,1)} %bitcast.32) | data formatting | bytes 16777216 | tf_op jit(solution)/shard_map/all_to_all | solution.py:35
  285.0 5.5 %convolution_convert_fusion.1 = bf16[128,2048]{1,0:T(8,128)(2,1)} fusion(bf16[2048,2048]{1,0:T(8,128)(2,1)} %bitcast.29, bf16[2048,128]{1,0:T(8,128)(2,1)S(1)} %select_reduce_fusion), kind=kOutput, calls=%fused_computation.6 | convolution fusion | flops 1074003968 | bytes 9437184 | tf_op jit(solution)/shard_map/dot_general | solution.py:39
  (10 shorter events, 0.0 us)
Async XLA Ops:
  0.0 5.1 %copy-start = (bf16[128,2048]{1,0:T(8,128)(2,1)S(1)}, bf16[128,2048]{1,0:T(8,128)(2,1)}, u32[]{:S(2)}) copy-start(bf16[128,2048]{1,0:T(8,128)(2,1)} %param.6) | copy-start | bytes 1572868
  160.6 5.1 %copy-start.2 = (bf16[128,10]{0,1:T(8,128)(2,1)S(1)}, bf16[128,10]{0,1:T(8,128)(2,1)}, u32[]{:S(2)}) copy-start(bf16[128,10]{0,1:T(8,128)(2,1)} %param.8) | copy-start | bytes 7684
  160.6 104.9 %all-to-all-start.1 = ((bf16[1,4,512,2048]{3,1,0,2:T(4,128)(2,1)}), bf16[1,4,512,2048]{3,1,0,2:T(4,128)(2,1)}, u32[]{:S(2)}, u32[]{:S(2)}) async-start(bf16[1,4,512,2048]{3,1,0,2:T(4,128)(2,1)} %copy.56), calls=%async_computation.1 | async-start | bytes 16777216 | tf_op jit(solution)/shard_map/all_to_all | solution.py:35
  285.0 5.5 %copy-start.1 = (bf16[128,2048]{1,0:T(8,128)(2,1)S(1)}, bf16[128,2048]{1,0:T(8,128)(2,1)}, u32[]{:S(2)}) copy-start(bf16[128,2048]{1,0:T(8,128)(2,1)} %param.6) | copy-start | bytes 1572868
where the time goes:
time: 296 us; the launch traced here: 291 us
  blocking collectives  104 us (35%)
  waiting for transfers between devices  98.7 us (33%)
  local copies, waits for them, and re-layouts  41.5 us (14%)
  matrix products  36.4 us (12%)
  starting transfers between devices  5.1 us (2%)
  other arithmetic  4.54 us (2%)
    all_to_all x1, blocking collectives, body(): lax.all_to_all(by_owner, 'ep', split_axis=0, concat_axis=2, tiled=True)  104 us
    all_to_all x1, waiting for transfers between devices, body(): lax.all_to_all(results[None], 'ep', split_axis=2, concat_axis=0, tiled=True)  98.7 us
    all_to_all x2, local copies, waits for them, and re-layouts, body(): lax.all_to_all(results[None], 'ep', split_axis=2, concat_axis=0, tiled=True)  19.5 us
    dot_general x1, matrix products, run_experts(): jnp.einsum('erf,edf->erd', hidden, down_w, preferred_element_type=jnp.flo...  16.4 us
    dot_general x1, matrix products, run_experts(): jnp.einsum('erd,edf->erf', rows, gate_w, preferred_element_type=jnp.float32)  12.2 us
    broadcast_in_dim x1, local copies, waits for them, and re-layouts, body(): results[None]  12.1 us
    all_to_all x1, local copies, waits for them, and re-layouts, body(): lax.all_to_all(by_owner, 'ep', split_axis=0, concat_axis=2, tiled=True)  8.27 us
  transfers between devices with their start and end apart: 1, of which 1 were waited for; matrix products, arithmetic and copies ran while one was open for 0% of the time, Pallas kernels for 0%

commit v1 on v0

v1 whole, which is shorter than its diff:
```python
import jax
import jax.numpy as jnp
from jax import lax
from jax.experimental import pallas as pl
from jax.experimental.pallas import tpu as pltpu
from jax.sharding import PartitionSpec as P

MESH = pl.DeviceIdType.MESH
F32, BF16 = jnp.float32, jnp.bfloat16
SIDE = 4
WIDTH, HIDDEN, TOKS, CAP, HELD = 2048, 512, 128, 16, 4
BODY, META = 1024, 16
ROWS = BODY + META
SPANS = {"f": (0, ROWS), "t": (0, 528), "b": (528, 512)}
RET = {"f": (0, BODY), "t": (0, 512), "b": (512, 512)}
ORDER = [(0, 0), (1, 0), (3, 0), (0, 1), (0, 3), (2, 0), (0, 2), (1, 1),
         (1, 3), (3, 1), (3, 3), (2, 1), (2, 3), (1, 2), (3, 2), (2, 2)]
SLOT = {d: i for i, d in enumerate(ORDER)}
CHUNK = 4
N_CHUNKS = len(ORDER) // CHUNK
SRC = 2 * CHUNK


def slot(h, df, dg):
    return SLOT[(df, dg)] if h == 0 else SLOT[(dg, df)]


def kernel(tok_hbm, meta_ref, wg_hbm, wu_hbm, wd_hbm, out_ref,
           g, p, wg, wu, wd, xb, ws, ps,
           own_sem, w_sem, ds, dr, xs, xr, ys, yr, rs, rr, free_sem, ready_sem):
    me = lax.axis_index("ep")
    core, x, y = me % 2, (me // 2) % SIDE, me // (2 * SIDE)

    def at(cx, cy, c):
        return (cy * SIDE + cx) * 2 + c

    nbr = {
        ("x", 1): at((x + 1) % SIDE, y, core),
        ("x", -1): at((x + SIDE - 1) % SIDE, y, core),
        ("y", 1): at(x, (y + 1) % SIDE, core),
        ("y", -1): at(x, (y + SIDE - 1) % SIDE, core),
    }
    mate = at(x, y, 1 - core)
    first, second = ("x", "y"), ("y", "x")

    own = []
    for h in range(2):
        for c in range(8):
            own.append(pltpu.make_async_copy(
                tok_hbm.at[:, pl.ds((h * 8 + c) * 128, 128)],
                g.at[0, 0, h, pl.ds(c * 128, 128), :], own_sem.at[h * 9 + c]))
        own.append(pltpu.make_async_copy(
            meta_ref.at[h], g.at[0, 0, h, pl.ds(BODY, META), :], own_sem.at[h * 9 + 8]))
    for c in own:
        c.start()
    loads = []
    for e in range(HELD):
        for i, (src, dst) in enumerate(((wg_hbm, wg), (wu_hbm, wu), (wd_hbm, wd))):
            loads.append(pltpu.make_async_copy(src.at[e], dst.at[e], w_sem.at[e * 3 + i]))
    for c in loads:
        c.start()

    barrier = pltpu.get_barrier_semaphore()
    for n in (*nbr.values(), mate):
        pl.semaphore_signal(barrier, inc=1, device_id={"ep": n}, device_id_type=MESH)
    pl.semaphore_wait(barrier, 5)
    for c in own:
        c.wait()

    ids, out_copies, pending_out = {}, {}, []

    def go(h, df, dg, part):
        key = (h, df, dg, part)
        ids[key] = i = len(ids)
        axis, d = (first[h], df) if dg == 0 else (second[h], dg)
        step = 1 if (d == 3 or part == "t") else -1
        prev = (d + step) % SIDE
        s = slot(h, prev, 0) if dg == 0 else slot(h, df, prev)
        a, n = SPANS[part]
        copy = pltpu.make_async_remote_copy(
            src_ref=g.at[0, s, h, pl.ds(a, n), :], dst_ref=g.at[0, slot(h, df, dg), h, pl.ds(a, n), :],
            send_sem=ds.at[i], recv_sem=dr.at[i],
            device_id={"ep": nbr[axis, step]}, device_id_type=MESH)
        copy.start()
        out_copies[key] = copy

    cross = {}

    def share(h, s):
        copy = pltpu.make_async_remote_copy(
            src_ref=g.at[0, s, h], dst_ref=g.at[1, s, h], send_sem=xs.at[h, s], recv_sem=xr.at[h, s],
            device_id={"ep": mate}, device_id_type=MESH)
        copy.start()
        cross[h, s] = copy

    def second_ring(h, df):
        go(h, df, 3, "f")
        go(h, df, 1, "f")

    def arrive(df, dg):
        for h in range(2):
            far = (df if dg == 0 else dg) == 2
            for part in ("t", "b") if far else ("f",):
                out_copies[h, df, dg, part].wait_recv()
            if dg == 0:
                if not far:
                    go(h, 2, 0, "t" if df == 3 else "b")
                second_ring(h, df)
            elif not far:
                go(h, df, 2, "t" if dg == 3 else "b")
            share(h, slot(h, df, dg))

    for h in range(2):
        go(h, 3, 0, "f")
        go(h, 1, 0, "f")
    for h in range(2):
        second_ring(h, 0)
    for h in range(2):
        share(h, 0)

    row_i = lax.broadcasted_iota(jnp.int32, (TOKS, TOKS), 0)
    col_i = lax.broadcasted_iota(jnp.int32, (TOKS, TOKS), 1)
    before = (row_i < col_i).astype(F32).astype(BF16)
    cap_i = lax.broadcasted_iota(jnp.int32, (CAP, TOKS), 0).astype(F32)
    back = {}

    def chunk(c):
        base = c * CHUNK
        for s in range(base, base + CHUNK):
            for h in range(2):
                cross[h, s].wait_recv()

        def route(i, carry):
            o, l = base + i // 2, i % 2
            chosen = g[l, o, 0, pl.ds(BODY, META), :].astype(F32)
            gate = g[l, o, 1, pl.ds(BODY, META), :].astype(F32)
            for e in range(HELD):
                mine = (me * HELD + e).astype(F32)
                ws[i, pl.ds(e, 1), :] = jnp.sum(jnp.where(chosen == mine, gate, 0.0), axis=0, keepdims=True)
            w = ws[i]
            rank = jnp.dot((w > 0.0).astype(F32).astype(BF16), before, preferred_element_type=F32)
            ps[i] = jnp.where(w > 0.0, rank, -1.0)
            r = ps[i]
            spread = jnp.concatenate(
                [jnp.where(jnp.broadcast_to(r[e:e + 1], (CAP, TOKS)) == cap_i, 1.0, 0.0) for e in range(HELD)],
                axis=0).astype(BF16)
            rows = pl.ds(pl.multiple_of(i * CAP, CAP), CAP)
            for j in range(8):
                h, k = j // 4, (j % 4) * 2
                pair = jnp.concatenate(
                    [g[l, o, h, pl.ds(k * 128, 128), :], g[l, o, h, pl.ds(k * 128 + 128, 128), :]], axis=1)
                picked = jnp.dot(spread, pair, preferred_element_type=F32).astype(BF16)
                for e in range(HELD):
                    xb[e, rows, pl.ds(j * 256, 256)] = picked[e * CAP:(e + 1) * CAP]
            return carry

        ws[...] = jnp.zeros_like(ws)
        lax.fori_loop(0, SRC, route, 0)
        pl.semaphore_signal(free_sem.at[c], inc=1, device_id={"ep": mate}, device_id_type=MESH)

        def expert(e, carry):
            rows = xb[e]
            gate_act = jnp.dot(rows, wg[e], preferred_element_type=F32)
            up_act = jnp.dot(rows, wu[e], preferred_element_type=F32)
            hidden = (gate_act / (1.0 + jnp.exp(-gate_act)) * up_act).astype(BF16)
            for j in range(4):
                xb[e, :, pl.ds(j * 512, 512)] = lax.dot_general(
                    hidden, wd[e, pl.ds(j * 512, 512), :], (((1,), (1,)), ((), ())),
                    preferred_element_type=F32).astype(BF16)
            return carry

        lax.fori_loop(0, HELD, expert, 0)

        def combine(i, carry):
            o, l = base + i // 2, i % 2
            r, w = ps[i], ws[i]
            mix = jnp.concatenate(
                [jnp.where(jnp.broadcast_to(r[e:e + 1], (CAP, TOKS)) == cap_i,
                           jnp.broadcast_to(w[e:e + 1], (CAP, TOKS)), 0.0) for e in range(HELD)], axis=0)
            mix = jnp.transpose(mix).astype(BF16)
            rows = pl.ds(pl.multiple_of(i * CAP, CAP), CAP)
            for j in range(8):
                h, k = j // 4, (j % 4) * 2
                res = jnp.concatenate([xb[e, rows, pl.ds(j * 256, 256)] for e in range(HELD)], axis=0)
                part = jnp.dot(mix, res, preferred_element_type=F32).astype(BF16)
                p[l, o, h, pl.ds(k * 128, 128), :] = part[:, :128]
                p[l, o, h, pl.ds(k * 128 + 128, 128), :] = part[:, 128:]
            return carry

        lax.fori_loop(0, SRC, combine, 0)
        pl.semaphore_wait(free_sem.at[c], 1)
        for s in range(base, base + CHUNK):
            copy = pltpu.make_async_remote_copy(
                src_ref=p.at[1, s], dst_ref=g.at[1, s, :, pl.ds(0, BODY), :],
                send_sem=ys.at[s], recv_sem=yr.at[s], device_id={"ep": mate}, device_id_type=MESH)
            copy.start()
            back[s] = copy

    arrive(1, 0)
    arrive(3, 0)
    arrive(0, 1)
    arrive(0, 3)
    for c in loads:
        c.wait()
    chunk(0)
    arrive(2, 0)
    arrive(1, 1)
    arrive(3, 1)
    arrive(1, 3)
    arrive(3, 3)
    arrive(0, 2)
    chunk(1)
    arrive(2, 1)
    arrive(1, 2)
    arrive(2, 3)
    chunk(2)
    arrive(3, 2)
    arrive(2, 2)
    chunk(3)

    for copy in (*out_copies.values(), *cross.values()):
        copy.wait_send()
    for n in nbr.values():
        pl.semaphore_signal(ready_sem, inc=1, device_id={"ep": n}, device_id_type=MESH)
    pl.semaphore_wait(ready_sem, 4)

    homes = {}

    def home(h, phase, df, kind):
        i = len(homes)
        axis = second[h] if phase == 1 else first[h]
        step = 1 if kind in "tp" else -1
        d = {"t": 2, "b": 2, "p": 1, "m": 3}[kind]
        s = slot(h, df, d) if phase == 1 else slot(h, d, 0)
        a, n = RET[kind if kind in "tb" else "f"]
        land = (df * 3 if phase == 1 else 12) + {"t": 0, "b": 0, "p": 1, "m": 2}[kind]
        copy = pltpu.make_async_remote_copy(
            src_ref=p.at[0, s, h, pl.ds(a, n), :], dst_ref=g.at[0, land, h, pl.ds(a, n), :],
            send_sem=rs.at[i], recv_sem=rr.at[i],
            device_id={"ep": nbr[axis, step]}, device_id_type=MESH)
        copy.start()
        homes[h, phase, df, kind] = copy

    came = set()

    def total(h, s, lands, mate_too=True):
        if mate_too and s not in came:
            back[s].wait_recv()
            came.add(s)
        for part in ("t", "b"):
            a, n = RET[part]
            terms = [k for k, span in lands if span in ("f", part)]
            if not mate_too and not terms:
                continue

            def add(i, carry):
                rows = pl.ds(pl.multiple_of(a + i * 128, 128), 128)
                v = p[0, s, h, rows, :].astype(F32)
                if mate_too:
                    v = v + g[1, s, h, rows, :].astype(F32)
                for k in terms:
                    v = v + g[0, k, h, rows, :].astype(F32)
                p[0, s, h, rows, :] = v.astype(BF16)
                return carry

            lax.fori_loop(0, n // 128, add, 0)

    def near(h, df):
        homes[h, 1, df, "t"].wait_recv()
        total(h, slot(h, df, 1), [(df * 3, "t")])
        home(h, 1, df, "p")
        homes[h, 1, df, "b"].wait_recv()
        total(h, slot(h, df, 3), [(df * 3, "b")])
        home(h, 1, df, "m")

    def column(h, df, more=()):
        homes[h, 1, df, "p"].wait_recv()
        homes[h, 1, df, "m"].wait_recv()
        total(h, slot(h, df, 0), [(df * 3 + 1, "f"), (df * 3 + 2, "f"), *more])

    for df in (2, 1, 3, 0):
        for h in range(2):
            total(h, slot(h, df, 2), [])
            home(h, 1, df, "t")
            home(h, 1, df, "b")
    for df in (2, 1, 3):
        for h in range(2):
            near(h, df)
    for h in range(2):
        column(h, 2)
        home(h, 2, 2, "t")
        home(h, 2, 2, "b")
    for h in range(2):
        near(h, 0)
    for h in range(2):
        homes[h, 2, 2, "t"].wait_recv()
        column(h, 1, [(12, "t")])
        home(h, 2, 1, "p")
        homes[h, 2, 2, "b"].wait_recv()
        column(h, 3, [(12, "b")])
        home(h, 2, 3, "m")
    for h in range(2):
        s = slot(h, 0, 0)
        for kind in ("p", "m"):
            homes[h, 1, 0, kind].wait_recv()
        homes[h, 2, 1, "p"].wait_recv()
        homes[h, 2, 3, "m"].wait_recv()
        if s not in came:
            back[s].wait_recv()
            came.add(s)
        for c in range(8):
            rows = pl.ds(c * 128, 128)
            v = p[0, s, h, rows, :].astype(F32) + g[1, s, h, rows, :].astype(F32)
            for k in (1, 2, 13, 14):
                v = v + g[0, k, h, rows, :].astype(F32)
            out_ref[:, pl.ds(h * BODY + c * 128, 128)] = v.astype(BF16)
    for copy in (*back.values(), *homes.values()):
        copy.wait_send()


def body(tokens, experts, gates, w_gate, w_up, w_down):
    chosen = jnp.pad(experts.astype(BF16).T, ((0, META - experts.shape[1]), (0, 0)), constant_values=-1)
    gate = jnp.pad(gates.T, ((0, META - gates.shape[1]), (0, 0)))
    meta = jnp.stack([chosen, gate])
    dma, any_spec = pltpu.SemaphoreType.DMA, pl.BlockSpec(memory_space=pl.ANY)
    vmem = pl.BlockSpec(memory_space=pltpu.VMEM)
    return pl.pallas_call(
        kernel,
        out_shape=jax.ShapeDtypeStruct((TOKS, WIDTH), BF16),
        in_specs=[any_spec, vmem, any_spec, any_spec, any_spec],
        out_specs=vmem,
        scratch_shapes=[
            pltpu.VMEM((2, 16, 2, ROWS, 128), BF16),
            pltpu.VMEM((2, 16, 2, BODY, 128), BF16),
            pltpu.VMEM((HELD, WIDTH, HIDDEN), BF16),
            pltpu.VMEM((HELD, WIDTH, HIDDEN), BF16),
            pltpu.VMEM((HELD, WIDTH, HIDDEN), BF16),
            pltpu.VMEM((HELD, SRC * CAP, WIDTH), BF16),
            pltpu.VMEM((SRC, 8, TOKS), F32),
            pltpu.VMEM((SRC, 8, TOKS), F32),
            dma((18,)), dma((12,)), dma((40,)), dma((40,)), dma((2, 16)), dma((2, 16)),
            dma((16,)), dma((16,)), dma((40,)), dma((40,)),
            pltpu.SemaphoreType.REGULAR((N_CHUNKS,)), pltpu.SemaphoreType.REGULAR,
        ],
        compiler_params=pltpu.CompilerParams(
            collective_id=0, has_side_effects=True, vmem_limit_bytes=67043328),
    )(tokens, meta, w_gate, w_up, w_down)


def solution(mesh):
    in_specs = (
        P(("rep", "ep"), None),
        P(("rep", "ep"), None),
        P(("rep", "ep"), None),
        P("ep", None, None),
        P("ep", None, None),
        P("ep", None, None),
    )
    out_specs = P(("rep", "ep"), None)
    return jax.shard_map(body, mesh=mesh, in_specs=in_specs, out_specs=out_specs, check_vma=False)
```

time: 296 us -> 143 us (0.48); the launches traced: 291 us -> 142 us
  Pallas kernels: 0 us -> 138 us
  blocking collectives: 104 us -> 0 us
  waiting for transfers between devices: 98.7 us -> 0 us
  local copies, waits for them, and re-layouts: 41.5 us -> 2.57 us
  matrix products: 36.4 us -> 0 us
  starting transfers between devices: 5.1 us -> 0 us
  other arithmetic: 4.54 us -> 1.3 us
    pallas_call x0 -> x1, Pallas kernels: none -> 138 us  [body(): pl.pallas_call(kernel, out_shape=jax.ShapeDtypeStruct((TOKS, WIDTH), BF16...]
    all_to_all x1 -> x0, blocking collectives: 104 us -> none  [body(): lax.all_to_all(by_owner, 'ep', split_axis=0, concat_axis=2, tiled=True)]
    all_to_all x1 -> x0, waiting for transfers between devices: 98.7 us -> none  [body(): lax.all_to_all(results[None], 'ep', split_axis=2, concat_axis=0, tiled=True)]
    dot_general x4 -> x0, matrix products: 36.4 us -> none  [the longest x1 16.4 us: run_experts(): jnp.einsum('erf,edf->erd', hidden, down_w, preferred_element_type=jnp.flo...]
    all_to_all x3 -> x0, local copies, waits for them, and re-layouts: 27.8 us -> none  [the longest x2 19.5 us: body(): lax.all_to_all(results[None], 'ep', split_axis=2, concat_axis=0, tiled=True)]
    broadcast_in_dim x1 -> x0, local copies, waits for them, and re-layouts: 12.1 us -> none  [body(): results[None]]
    all_to_all x1 -> x0, starting transfers between devices: 5.1 us -> none  [body(): lax.all_to_all(results[None], 'ep', split_axis=2, concat_axis=0, tiled=True)]
  transfers between devices with their start and end apart: 1 -> 0, of which waited for: 1 -> 0; matrix products, arithmetic and copies ran while one was open for 0% -> 0% of each run, Pallas kernels for 0% -> 0%
where the time goes in v1:
time: 143 us; the launch traced here: 142 us
  Pallas kernels  138 us (97%)
  local copies, waits for them, and re-layouts  2.57 us (2%)
    pallas_call x1, Pallas kernels, body(): pl.pallas_call(kernel, out_shape=jax.ShapeDtypeStruct((TOKS, WIDTH), BF16...  138 us

profile of v1, /device:TPU:1, one launch (start us, length us, event | category | flops | bytes accessed | tf_op | source)
XLA Modules:
  0.0 142.4 jit_solution(9252287042151927078)
XLA Ops:
  0.0 0.7 convert_bitcast_fusion
  0.7 0.7 pad_bitcast_fusion
  1.4 0.6 pad_maximum_fusion.meta_ref
  2.0 138.5 %shard_map.64 = bf16[128,2048]{1,0:T(8,128)(2,1)} custom-call(bf16[128,2048]{1,0:T(8,128)(2,1)} %tok_hbm.1, bf16[2,16,128]{2,1,0:T(8,128)(2,1)} %pad_maximum_fusion.meta_ref, bf16[4,2048,512]{2,1,0:T(8,128)(2,1)} %wg_hbm.1, bf16[4,2048,512]{2,1,0:T(8,128)(2,1)} %wu_hbm.1, bf16[4,2048,512]{2,1,0:T(8,128)(2,1)} %wd_hbm.1), custom_call_target="tpu_custom_call" | custom-call | tf_op jit(solution)/shard_map/pallas_call | solution.py:327
  140.5 1.9 %copy.8 = bf16[128,2048]{1,0:T(8,128)(2,1)} copy(bf16[128,2048]{1,0:T(8,128)(2,1)} %shard_map.64) | data formatting | bytes 1048576

commit v2 on v0

v2 whole, which is shorter than its diff:
```python
import jax
import jax.numpy as jnp
from jax import lax
from jax.experimental import pallas as pl
from jax.experimental.pallas import tpu as pltpu
from jax.sharding import PartitionSpec as P

MESH = pl.DeviceIdType.MESH
F32, BF16 = jnp.float32, jnp.bfloat16
SIDE = 4
WIDTH, HIDDEN, TOKS, CAP, HELD = 2048, 512, 128, 16, 4
HALF = WIDTH // 2
BODY, META = 1024, 16
ROWS = BODY + META
SPANS = {"f": (0, ROWS), "t": (0, 528), "b": (528, 512)}
RET = {"f": (0, BODY), "t": (0, 512), "b": (512, 512)}
ORDER = [(0, 0), (1, 0), (3, 0), (0, 1), (0, 3), (1, 1), (1, 3), (3, 1),
         (3, 3), (2, 0), (0, 2), (2, 1), (2, 3), (1, 2), (3, 2), (2, 2)]
SLOT = {d: i for i, d in enumerate(ORDER)}
CHIPS = len(ORDER)


def kernel(tok_hbm, meta_ref, wg_hbm, wu_hbm, wd_hbm, out_hbm,
           g, p, wg, wu, wd, xb, ws, ps, fin,
           own_sem, w_sem, os_, or_, ds, dr, xs, xr, ys, yr, rs, rr, fs, fr, o_sem, free_sem, ready_sem):
    me = lax.axis_index("ep")
    core, x, y = me % 2, (me // 2) % SIDE, me // (2 * SIDE)
    other = 1 - core

    def at(cx, cy, c):
        return (cy * SIDE + cx) * 2 + c

    def pick(along_x, along_y):
        return other * along_x + core * along_y

    xp, xm = at((x + 1) % SIDE, y, core), at((x + SIDE - 1) % SIDE, y, core)
    yp, ym = at(x, (y + 1) % SIDE, core), at(x, (y + SIDE - 1) % SIDE, core)
    nbr = {("f", 1): pick(xp, yp), ("f", -1): pick(xm, ym), ("g", 1): pick(yp, xp), ("g", -1): pick(ym, xm)}
    mate = at(x, y, other)

    def remote(src, dst, send, recv, n):
        return pltpu.make_async_remote_copy(
            src_ref=src, dst_ref=dst, send_sem=send, recv_sem=recv, device_id={"ep": n}, device_id_type=MESH)

    own = []
    for k, half in ((0, core), (1, other)):
        for c in range(8):
            own.append(pltpu.make_async_copy(
                tok_hbm.at[:, pl.ds(pl.multiple_of(half * HALF + c * 128, 128), 128)],
                g.at[core, k, 0, pl.ds(c * 128, 128), :], own_sem.at[k * 9 + c]))
        own.append(pltpu.make_async_copy(
            meta_ref.at[half], g.at[core, k, 0, pl.ds(BODY, META), :], own_sem.at[k * 9 + 8]))
    for c in own:
        c.start()
    loads = []
    for e in range(HELD):
        for i, (src, dst) in enumerate(((wg_hbm, wg), (wu_hbm, wu), (wd_hbm, wd))):
            loads.append(pltpu.make_async_copy(src.at[e], dst.at[e], w_sem.at[e * 3 + i]))
    for c in loads:
        c.start()

    barrier = pltpu.get_barrier_semaphore()
    for n in (*nbr.values(), mate):
        pl.semaphore_signal(barrier, inc=1, device_id={"ep": n}, device_id_type=MESH)
    pl.semaphore_wait(barrier, 5)
    for c in own:
        c.wait()
    halves = [remote(g.at[core, 1 - k, 0], g.at[core, k, 0], os_.at[k], or_.at[k], mate) for k in range(2)]
    for c in halves:
        c.start()

    out_ids, sent, crossed = {}, {0: [], 1: []}, {0: [], 1: []}

    def leg(b, df, dg, part):
        i = out_ids.setdefault((df, dg, part), len(out_ids))
        axis, d = ("f", df) if dg == 0 else ("g", dg)
        step = 1 if (d == 3 or part == "t") else -1
        prev = (d + step) % SIDE
        s = SLOT[(prev, 0) if dg == 0 else (df, prev)]
        a, n = SPANS[part]
        return remote(g.at[b, 0, s, pl.ds(a, n), :], g.at[b, 0, SLOT[df, dg], pl.ds(a, n), :],
                      ds.at[b, i], dr.at[b, i], nbr[axis, step])

    def go(b, *key):
        copy = leg(b, *key)
        copy.start()
        sent[b].append(copy)

    def share(b, df, dg):
        return remote(g.at[b, 0, SLOT[df, dg]], g.at[b, 1, SLOT[dg, df]],
                      xs.at[b, SLOT[dg, df]], xr.at[b, SLOT[dg, df]], mate)

    def second_ring(b, df):
        go(b, df, 3, "f")
        go(b, df, 1, "f")

    def first_ring(b):
        go(b, 3, 0, "f")
        go(b, 1, 0, "f")

    def arrive(b, df, dg):
        far = (df if dg == 0 else dg) == 2
        for part in ("t", "b") if far else ("f",):
            leg(b, df, dg, part).wait_recv()
        if dg == 0:
            if not far:
                go(b, 2, 0, "t" if df == 3 else "b")
            second_ring(b, df)
        elif not far:
            go(b, df, 2, "t" if dg == 3 else "b")
        copy = share(b, df, dg)
        copy.start()
        crossed[b].append(copy)

    row_i = lax.broadcasted_iota(jnp.int32, (TOKS, TOKS), 0)
    col_i = lax.broadcasted_iota(jnp.int32, (TOKS, TOKS), 1)
    before = (row_i < col_i).astype(F32).astype(BF16)
    cap_i = lax.broadcasted_iota(jnp.int32, (CAP, TOKS), 0).astype(F32)

    def rows_of(s):
        return pl.ds(pl.multiple_of(s * CAP, CAP), CAP)

    def route(b, s0, n):
        for s in range(s0, s0 + n):
            if s > 0:
                df, dg = ORDER[s]
                share(b, dg, df).wait_recv()

        def one(s, carry):
            chosen = g[b, core, s, pl.ds(BODY, META), :].astype(F32)
            gate = g[b, other, s, pl.ds(BODY, META), :].astype(F32)
            for e in range(HELD):
                mine = (me * HELD + e).astype(F32)
                ws[s, pl.ds(e, 1), :] = jnp.sum(jnp.where(chosen == mine, gate, 0.0), axis=0, keepdims=True)
            w = ws[s]
            rank = jnp.dot((w > 0.0).astype(F32).astype(BF16), before, preferred_element_type=F32)
            r = jnp.where(w > 0.0, rank, -1.0)
            ps[s] = r
            spread = jnp.concatenate(
                [jnp.where(jnp.broadcast_to(r[e:e + 1], (CAP, TOKS)) == cap_i, 1.0, 0.0) for e in range(HELD)],
                axis=0).astype(BF16)
            for j in range(8):
                k, c = (j // 4 + core) % 2, (j % 4) * 2
                pair = jnp.concatenate(
                    [g[b, k, s, pl.ds(c * 128, 128), :], g[b, k, s, pl.ds(c * 128 + 128, 128), :]], axis=1)
                picked = jnp.dot(spread, pair, preferred_element_type=F32).astype(BF16)
                for e in range(HELD):
                    xb[e, rows_of(s), pl.ds(j * 256, 256)] = picked[e * CAP:(e + 1) * CAP]
            return carry

        lax.fori_loop(s0, s0 + n, one, 0)

    def expert(e0, n):
        def one(e, carry):
            rows = xb[e]
            gate_act = jnp.dot(rows, wg[e], preferred_element_type=F32)
            up_act = jnp.dot(rows, wu[e], preferred_element_type=F32)
            hidden = (gate_act / (1.0 + jnp.exp(-gate_act)) * up_act).astype(BF16)
            for j in range(4):
                xb[e, :, pl.ds(j * 512, 512)] = lax.dot_general(
                    hidden, wd[e, pl.ds(j * 512, 512), :], (((1,), (1,)), ((), ())),
                    preferred_element_type=F32).astype(BF16)
            return carry

        lax.fori_loop(e0, e0 + n, one, 0)

    backs = {0: [], 1: []}

    def back(b, df, dg):
        return remote(p.at[b, 1, SLOT[df, dg]], g.at[b, 1, SLOT[dg, df], pl.ds(0, BODY), :],
                      ys.at[b, SLOT[dg, df]], yr.at[b, SLOT[dg, df]], mate)

    def combine(b, s0, n):
        def one(s, carry):
            r, w = ps[s], ws[s]
            mix = jnp.concatenate(
                [jnp.where(jnp.broadcast_to(r[e:e + 1], (CAP, TOKS)) == cap_i,
                           jnp.broadcast_to(w[e:e + 1], (CAP, TOKS)), 0.0) for e in range(HELD)], axis=0)
            mix = jnp.transpose(mix).astype(BF16)
            for j in range(8):
                k, c = (j // 4 + core) % 2, (j % 4) * 2
                res = jnp.concatenate([xb[e, rows_of(s), pl.ds(j * 256, 256)] for e in range(HELD)], axis=0)
                part = jnp.dot(mix, res, preferred_element_type=F32).astype(BF16)
                p[b, k, s, pl.ds(c * 128, 128), :] = part[:, :128]
                p[b, k, s, pl.ds(c * 128 + 128, 128), :] = part[:, 128:]
            return carry

        lax.fori_loop(s0, s0 + n, one, 0)
        if not backs[b]:
            pl.semaphore_wait(free_sem.at[b], 1)
        for s in range(s0, s0 + n):
            copy = back(b, *ORDER[s])
            copy.start()
            backs[b].append(copy)

    def mate_free(b):
        pl.semaphore_signal(free_sem.at[b], inc=1, device_id={"ep": mate}, device_id_type=MESH)

    def ready(b):
        for copy in (*sent[b], *crossed[b]):
            copy.wait_send()
        for n in nbr.values():
            pl.semaphore_signal(ready_sem.at[b], inc=1, device_id={"ep": n}, device_id_type=MESH)

    home_ids, homes = {}, []

    def hop(b, phase, df, kind):
        i = home_ids.setdefault((phase, df, kind), len(home_ids))
        step = 1 if kind in "tp" else -1
        d = {"t": 2, "b": 2, "p": 1, "m": 3}[kind]
        s = SLOT[(df, d) if phase == 1 else (d, 0)]
        a, n = RET[kind if kind in "tb" else "f"]
        land = (df * 3 if phase == 1 else 12) + {"t": 0, "b": 0, "p": 1, "m": 2}[kind]
        return remote(p.at[b, 0, s, pl.ds(a, n), :], g.at[b, 0, land, pl.ds(a, n), :],
                      rs.at[b, i], rr.at[b, i], nbr["g" if phase == 1 else "f", step])

    def home(*key):
        copy = hop(*key)
        copy.start()
        homes.append(copy)

    def total(b, df, dg, lands):
        s = SLOT[df, dg]
        back(b, dg, df).wait_recv()
        for part in ("t", "b"):
            a, n = RET[part]
            terms = [k for k, span in lands if span in ("f", part)]

            def add(i, carry):
                rows = pl.ds(pl.multiple_of(a + i * 128, 128), 128)
                v = p[b, 0, s, rows, :].astype(F32) + g[b, 1, s, rows, :].astype(F32)
                for k in terms:
                    v = v + g[b, 0, k, rows, :].astype(F32)
                p[b, 0, s, rows, :] = v.astype(BF16)
                return carry

            lax.fori_loop(0, n // 128, add, 0)

    def far(b, df):
        total(b, df, 2, [])
        home(b, 1, df, "t")
        home(b, 1, df, "b")

    def near(b, df):
        hop(b, 1, df, "t").wait_recv()
        total(b, df, 1, [(df * 3, "t")])
        home(b, 1, df, "p")
        hop(b, 1, df, "b").wait_recv()
        total(b, df, 3, [(df * 3, "b")])
        home(b, 1, df, "m")

    def column(b, df):
        hop(b, 1, df, "p").wait_recv()
        hop(b, 1, df, "m").wait_recv()
        lands = [(df * 3 + 1, "f"), (df * 3 + 2, "f")]
        kind = {1: "t", 3: "b"}.get(df)
        if kind:
            hop(b, 2, 2, kind).wait_recv()
            lands.append((12, kind))
        if df == 0:
            hop(b, 2, 1, "p").wait_recv()
            hop(b, 2, 3, "m").wait_recv()
            lands += [(13, "f"), (14, "f")]
        total(b, df, 0, lands)
        if df == 2:
            home(b, 2, 2, "t")
            home(b, 2, 2, "b")
        elif df:
            home(b, 2, df, "p" if df == 1 else "m")

    def store(src, half, i):
        return [pltpu.make_async_copy(
            src.at[pl.ds(c * 128, 128), :],
            out_hbm.at[:, pl.ds(pl.multiple_of(half * HALF + c * 128, 128), 128)], o_sem.at[i * 8 + c]) for c in range(8)]

    handover = remote(p.at[other, 0, 0], fin, fs, fr, mate)

    def finish(b):
        column(b, 0)

        @pl.when(core == b)
        def _():
            for c in store(p.at[b, 0, 0], core, 0):
                c.start()

        @pl.when(core != b)
        def _():
            handover.start()

    ws[...] = jnp.zeros_like(ws)
    for c in halves:
        c.wait_recv()
    first_ring(0)
    for c in sent[0]:
        c.wait_send()
    sent[0].clear()
    second_ring(0, 0)
    arrive(0, 1, 0)
    arrive(0, 3, 0)
    first_ring(1)
    arrive(0, 0, 1)
    arrive(0, 0, 3)
    arrive(0, 2, 0)
    route(0, 0, 5)
    arrive(0, 1, 1)
    arrive(0, 1, 3)
    arrive(0, 3, 1)
    arrive(0, 3, 3)
    arrive(0, 0, 2)
    route(0, 5, 4)
    arrive(0, 2, 1)
    arrive(0, 2, 3)
    second_ring(1, 0)
    arrive(1, 1, 0)
    arrive(1, 3, 0)
    route(0, 9, 2)
    arrive(0, 1, 2)
    arrive(0, 3, 2)
    arrive(0, 2, 2)
    route(0, 11, 5)
    for c in halves:
        c.wait_send()
    mate_free(0)
    for c in loads:
        c.wait()
    expert(0, 1)
    arrive(1, 0, 1)
    arrive(1, 0, 3)
    arrive(1, 2, 0)
    expert(1, 1)
    ready(0)
    arrive(1, 1, 1)
    arrive(1, 1, 3)
    expert(2, 1)
    arrive(1, 3, 1)
    arrive(1, 3, 3)
    arrive(1, 0, 2)
    expert(3, 1)
    combine(0, 9, 7)
    arrive(1, 2, 1)
    arrive(1, 2, 3)
    combine(0, 0, 4)
    pl.semaphore_wait(ready_sem.at[0], 4)
    for df in (2, 1, 3, 0):
        far(0, df)
    combine(0, 4, 5)
    arrive(1, 1, 2)
    arrive(1, 3, 2)
    arrive(1, 2, 2)
    route(1, 0, 9)
    near(0, 2)
    route(1, 9, 7)
    mate_free(1)
    near(0, 1)
    near(0, 3)
    near(0, 0)
    expert(0, 2)
    ready(1)
    column(0, 2)
    expert(2, 2)
    column(0, 1)
    column(0, 3)
    combine(1, 9, 7)
    combine(1, 0, 4)
    pl.semaphore_wait(ready_sem.at[1], 4)
    for df in (2, 1, 3, 0):
        far(1, df)
    combine(1, 4, 5)
    finish(0)
    for df in (2, 1, 3):
        near(1, df)
    column(1, 2)
    near(1, 0)
    column(1, 1)
    column(1, 3)
    finish(1)
    handover.wait_recv()
    rest = store(fin, other, 1)
    for c in rest:
        c.start()
    for copy in (*backs[0], *backs[1], *homes):
        copy.wait_send()
    handover.wait_send()
    for c in (*store(p.at[core, 0, 0], core, 0), *rest):
        c.wait()


def body(tokens, experts, gates, w_gate, w_up, w_down):
    chosen = jnp.pad(experts.astype(BF16).T, ((0, META - experts.shape[1]), (0, 0)), constant_values=-1)
    gate = jnp.pad(gates.T, ((0, META - gates.shape[1]), (0, 0)))
    meta = jnp.stack([chosen, gate])
    dma, any_spec = pltpu.SemaphoreType.DMA, pl.BlockSpec(memory_space=pl.ANY)
    vmem = pl.BlockSpec(memory_space=pltpu.VMEM)
    return pl.pallas_call(
        kernel,
        out_shape=jax.ShapeDtypeStruct((TOKS, WIDTH), BF16),
        in_specs=[any_spec, vmem, any_spec, any_spec, any_spec],
        out_specs=any_spec,
        scratch_shapes=[
            pltpu.VMEM((2, 2, CHIPS, ROWS, 128), BF16),
            pltpu.VMEM((2, 2, CHIPS, BODY, 128), BF16),
            pltpu.VMEM((HELD, WIDTH, HIDDEN), BF16),
            pltpu.VMEM((HELD, WIDTH, HIDDEN), BF16),
            pltpu.VMEM((HELD, WIDTH, HIDDEN), BF16),
            pltpu.VMEM((HELD, CHIPS * CAP, WIDTH), BF16),
            pltpu.VMEM((CHIPS, 8, TOKS), F32),
            pltpu.VMEM((CHIPS, 8, TOKS), F32),
            pltpu.VMEM((BODY, 128), BF16),
            dma((18,)), dma((12,)), dma((2,)), dma((2,)),
            dma((2, 20)), dma((2, 20)), dma((2, 16)), dma((2, 16)), dma((2, 16)), dma((2, 16)),
            dma((2, 20)), dma((2, 20)), dma, dma, dma((16,)),
            pltpu.SemaphoreType.REGULAR((2,)), pltpu.SemaphoreType.REGULAR((2,)),
        ],
        compiler_params=pltpu.CompilerParams(
            collective_id=0, has_side_effects=True, vmem_limit_bytes=67043328),
    )(tokens, meta, w_gate, w_up, w_down)


def solution(mesh):
    in_specs = (
        P(("rep", "ep"), None),
        P(("rep", "ep"), None),
        P(("rep", "ep"), None),
        P("ep", None, None),
        P("ep", None, None),
        P("ep", None, None),
    )
    out_specs = P(("rep", "ep"), None)
    return jax.shard_map(body, mesh=mesh, in_specs=in_specs, out_specs=out_specs, check_vma=False)
```

time: 296 us -> 114 us (0.39); the launches traced: 291 us -> 113 us
  Pallas kernels: 0 us -> 110 us
  blocking collectives: 104 us -> 0 us
  waiting for transfers between devices: 98.7 us -> 0 us
  local copies, waits for them, and re-layouts: 41.5 us -> 2.57 us
  matrix products: 36.4 us -> 0 us
  starting transfers between devices: 5.1 us -> 0 us
  other arithmetic: 4.54 us -> 1.3 us
    pallas_call x0 -> x1, Pallas kernels: none -> 110 us  [body(): pl.pallas_call(kernel, out_shape=jax.ShapeDtypeStruct((TOKS, WIDTH), BF16...]
    all_to_all x1 -> x0, blocking collectives: 104 us -> none  [body(): lax.all_to_all(by_owner, 'ep', split_axis=0, concat_axis=2, tiled=True)]
    all_to_all x1 -> x0, waiting for transfers between devices: 98.7 us -> none  [body(): lax.all_to_all(results[None], 'ep', split_axis=2, concat_axis=0, tiled=True)]
    dot_general x4 -> x0, matrix products: 36.4 us -> none  [the longest x1 16.4 us: run_experts(): jnp.einsum('erf,edf->erd', hidden, down_w, preferred_element_type=jnp.flo...]
    all_to_all x3 -> x0, local copies, waits for them, and re-layouts: 27.8 us -> none  [the longest x2 19.5 us: body(): lax.all_to_all(results[None], 'ep', split_axis=2, concat_axis=0, tiled=True)]
    broadcast_in_dim x1 -> x0, local copies, waits for them, and re-layouts: 12.1 us -> none  [body(): results[None]]
    all_to_all x1 -> x0, starting transfers between devices: 5.1 us -> none  [body(): lax.all_to_all(results[None], 'ep', split_axis=2, concat_axis=0, tiled=True)]
  transfers between devices with their start and end apart: 1 -> 0, of which waited for: 1 -> 0; matrix products, arithmetic and copies ran while one was open for 0% -> 0% of each run, Pallas kernels for 0% -> 0%
where the time goes in v2:
time: 114 us; the launch traced here: 113 us
  Pallas kernels  110 us (96%)
  local copies, waits for them, and re-layouts  2.57 us (2%)
  other arithmetic  1.3 us (1%)
    pallas_call x1, Pallas kernels, body(): pl.pallas_call(kernel, out_shape=jax.ShapeDtypeStruct((TOKS, WIDTH), BF16...  110 us

profile of v2, /device:TPU:1, one launch (start us, length us, event | category | flops | bytes accessed | tf_op | source)
XLA Modules:
  0.0 113.5 jit_solution(13239756385401231665)
XLA Ops:
  0.0 0.7 convert_bitcast_fusion
  0.7 0.7 pad_bitcast_fusion
  1.4 0.6 pad_maximum_fusion.meta_ref
  2.0 109.6 %shard_map.64 = bf16[128,2048]{1,0:T(8,128)(2,1)} custom-call(bf16[128,2048]{1,0:T(8,128)(2,1)} %tok_hbm.1, bf16[2,16,128]{2,1,0:T(8,128)(2,1)} %pad_maximum_fusion.meta_ref, bf16[4,2048,512]{2,1,0:T(8,128)(2,1)} %wg_hbm.1, bf16[4,2048,512]{2,1,0:T(8,128)(2,1)} %wu_hbm.1, bf16[4,2048,512]{2,1,0:T(8,128)(2,1)} %wd_hbm.1), custom_call_target="tpu_custom_call" | custom-call | tf_op jit(solution)/shard_map/pallas_call | solution.py:394
  111.6 1.9 %copy.8 = bf16[128,2048]{1,0:T(8,128)(2,1)} copy(bf16[128,2048]{1,0:T(8,128)(2,1)} %shard_map.64) | data formatting | bytes 1048576

commit v3 on v2

--- a/solution.py
+++ b/solution.py
@@ -20,9 +20,9 @@
 CHIPS = len(ORDER)
 
 
-def kernel(tok_hbm, meta_ref, wg_hbm, wu_hbm, wd_hbm, out_hbm,
+def kernel(tok_hbm, chosen_hbm, gates_hbm, wg_hbm, wu_hbm, wd_hbm, out_hbm,
            g, p, wg, wu, wd, xb, ws, ps, fin,
-           own_sem, w_sem, os_, or_, ds, dr, xs, xr, ys, yr, rs, rr, fs, fr, o_sem, free_sem, ready_sem):
+           ids_v, gates_v, rows_v, own_sem, w_sem, os_, or_, ds, dr, xs, xr, ys, yr, rs, rr, fs, fr, o_sem, free_sem, ready_sem):
     me = lax.axis_index("ep")
     core, x, y = me % 2, (me // 2) % SIDE, me // (2 * SIDE)
     other = 1 - core
@@ -48,20 +48,26 @@
             own.append(pltpu.make_async_copy(
                 tok_hbm.at[:, pl.ds(pl.multiple_of(half * HALF + c * 128, 128), 128)],
                 g.at[core, k, 0, pl.ds(c * 128, 128), :], own_sem.at[k * 9 + c]))
-        own.append(pltpu.make_async_copy(
-            meta_ref.at[half], g.at[core, k, 0, pl.ds(BODY, META), :], own_sem.at[k * 9 + 8]))
-    for c in own:
+    routing = [pltpu.make_async_copy(chosen_hbm, ids_v, own_sem.at[8]), pltpu.make_async_copy(gates_hbm, gates_v, own_sem.at[17])]
+    for c in (*routing, *own):
         c.start()
     loads = []
     for e in range(HELD):
         for i, (src, dst) in enumerate(((wg_hbm, wg), (wu_hbm, wu), (wd_hbm, wd))):
             loads.append(pltpu.make_async_copy(src.at[e], dst.at[e], w_sem.at[e * 3 + i]))
-    for c in loads:
-        c.start()
-
     barrier = pltpu.get_barrier_semaphore()
     for n in (*nbr.values(), mate):
         pl.semaphore_signal(barrier, inc=1, device_id={"ep": n}, device_id_type=MESH)
+    ws[...] = jnp.zeros_like(ws)
+    topk = ids_v.shape[0]
+    rows_v[0] = jnp.full((META, TOKS), -1.0, F32)
+    rows_v[1] = jnp.zeros((META, TOKS), F32)
+    for c in routing:
+        c.wait()
+    rows_v[0, pl.ds(0, topk), :] = ids_v[...].astype(F32)
+    rows_v[1, pl.ds(0, topk), :] = gates_v[...].astype(F32)
+    g[core, core, 0, pl.ds(BODY, META), :] = rows_v[0].astype(BF16)
+    g[core, other, 0, pl.ds(BODY, META), :] = rows_v[1].astype(BF16)
     pl.semaphore_wait(barrier, 5)
     for c in own:
         c.wait()
@@ -74,7 +80,7 @@
     def leg(b, df, dg, part):
         i = out_ids.setdefault((df, dg, part), len(out_ids))
         axis, d = ("f", df) if dg == 0 else ("g", dg)
-        step = 1 if (d == 3 or part == "t") else -1
+        step = 1 if d == 3 or (d == 2 and part == "t") else -1
         prev = (d + step) % SIDE
         s = SLOT[(prev, 0) if dg == 0 else (df, prev)]
         a, n = SPANS[part]
@@ -95,19 +101,23 @@
         go(b, df, 1, "f")
 
     def first_ring(b):
-        go(b, 3, 0, "f")
-        go(b, 1, 0, "f")
+        go(b, 3, 0, "t")
+        go(b, 1, 0, "b")
+        go(b, 3, 0, "b")
+        go(b, 1, 0, "t")
 
     def arrive(b, df, dg):
-        far = (df if dg == 0 else dg) == 2
-        for part in ("t", "b") if far else ("f",):
-            leg(b, df, dg, part).wait_recv()
         if dg == 0:
-            if not far:
-                go(b, 2, 0, "t" if df == 3 else "b")
+            for part in ("b", "t") if df == 1 else ("t", "b"):
+                leg(b, df, 0, part).wait_recv()
+                if (df, part) in ((3, "t"), (1, "b")):
+                    go(b, 2, 0, part)
             second_ring(b, df)
-        elif not far:
-            go(b, df, 2, "t" if dg == 3 else "b")
+        else:
+            for part in ("t", "b") if dg == 2 else ("f",):
+                leg(b, df, dg, part).wait_recv()
+            if dg != 2:
+                go(b, df, 2, "t" if dg == 3 else "b")
         copy = share(b, df, dg)
         copy.start()
         crossed[b].append(copy)
@@ -287,14 +297,15 @@
         def _():
             handover.start()
 
-    ws[...] = jnp.zeros_like(ws)
     for c in halves:
         c.wait_recv()
     first_ring(0)
-    for c in sent[0]:
+    for c in sent[0][:2]:
         c.wait_send()
-    sent[0].clear()
+    del sent[0][:2]
     second_ring(0, 0)
+    for c in loads:
+        c.start()
     arrive(0, 1, 0)
     arrive(0, 3, 0)
     first_ring(1)
@@ -336,41 +347,50 @@
     arrive(1, 3, 3)
     arrive(1, 0, 2)
     expert(3, 1)
-    combine(0, 9, 7)
+    combine(0, 11, 5)
+    combine(0, 9, 2)
     arrive(1, 2, 1)
     arrive(1, 2, 3)
-    combine(0, 0, 4)
+    combine(0, 5, 4)
     pl.semaphore_wait(ready_sem.at[0], 4)
-    for df in (2, 1, 3, 0):
-        far(0, df)
-    combine(0, 4, 5)
+    far(0, 2)
+    far(0, 1)
+    far(0, 3)
+    combine(0, 0, 5)
     arrive(1, 1, 2)
     arrive(1, 3, 2)
     arrive(1, 2, 2)
-    route(1, 0, 9)
+    far(0, 0)
+    route(1, 0, 5)
     near(0, 2)
+    route(1, 5, 4)
+    near(0, 1)
+    near(0, 3)
     route(1, 9, 7)
     mate_free(1)
-    near(0, 1)
-    near(0, 3)
     near(0, 0)
-    expert(0, 2)
+    expert(0, 1)
     ready(1)
+    expert(1, 1)
     column(0, 2)
     expert(2, 2)
     column(0, 1)
     column(0, 3)
-    combine(1, 9, 7)
-    combine(1, 0, 4)
+    combine(1, 11, 5)
+    combine(1, 9, 2)
     pl.semaphore_wait(ready_sem.at[1], 4)
-    for df in (2, 1, 3, 0):
-        far(1, df)
-    combine(1, 4, 5)
-    finish(0)
-    for df in (2, 1, 3):
-        near(1, df)
+    far(1, 2)
+    far(1, 1)
+    far(1, 3)
+    far(1, 0)
+    combine(1, 5, 4)
+    near(1, 2)
+    combine(1, 0, 5)
+    near(1, 1)
+    near(1, 3)
     column(1, 2)
     near(1, 0)
+    finish(0)
     column(1, 1)
     column(1, 3)
     finish(1)
@@ -386,15 +406,11 @@
 
 
 def body(tokens, experts, gates, w_gate, w_up, w_down):
-    chosen = jnp.pad(experts.astype(BF16).T, ((0, META - experts.shape[1]), (0, 0)), constant_values=-1)
-    gate = jnp.pad(gates.T, ((0, META - gates.shape[1]), (0, 0)))
-    meta = jnp.stack([chosen, gate])
     dma, any_spec = pltpu.SemaphoreType.DMA, pl.BlockSpec(memory_space=pl.ANY)
-    vmem = pl.BlockSpec(memory_space=pltpu.VMEM)
     return pl.pallas_call(
         kernel,
         out_shape=jax.ShapeDtypeStruct((TOKS, WIDTH), BF16),
-        in_specs=[any_spec, vmem, any_spec, any_spec, any_spec],
+        in_specs=[any_spec] * 6,
         out_specs=any_spec,
         scratch_shapes=[
             pltpu.VMEM((2, 2, CHIPS, ROWS, 128), BF16),
@@ -406,14 +422,17 @@
             pltpu.VMEM((CHIPS, 8, TOKS), F32),
             pltpu.VMEM((CHIPS, 8, TOKS), F32),
             pltpu.VMEM((BODY, 128), BF16),
+            pltpu.VMEM((experts.shape[1], TOKS), jnp.int32),
+            pltpu.VMEM((gates.shape[1], TOKS), BF16),
+            pltpu.VMEM((2, META, TOKS), F32),
             dma((18,)), dma((12,)), dma((2,)), dma((2,)),
-            dma((2, 20)), dma((2, 20)), dma((2, 16)), dma((2, 16)), dma((2, 16)), dma((2, 16)),
+            dma((2, 22)), dma((2, 22)), dma((2, 16)), dma((2, 16)), dma((2, 16)), dma((2, 16)),
             dma((2, 20)), dma((2, 20)), dma, dma, dma((16,)),
             pltpu.SemaphoreType.REGULAR((2,)), pltpu.SemaphoreType.REGULAR((2,)),
         ],
         compiler_params=pltpu.CompilerParams(
             collective_id=0, has_side_effects=True, vmem_limit_bytes=67043328),
-    )(tokens, meta, w_gate, w_up, w_down)
+    )(tokens, experts.T, gates.T, w_gate, w_up, w_down)
 
 
 def solution(mesh):

time: 114 us -> 109 us (0.956)
  Pallas kernels: 110 us -> 107 us
  other arithmetic: 1.3 us -> 0 us
    pallas_call x1, Pallas kernels: 110 us -> 107 us  [body(): pl.pallas_call(kernel, out_shape=jax.ShapeDtypeStruct((TOKS, WIDTH), BF16...]
where the time goes in v3:
time: 109 us; the launch traced here: 108 us
  Pallas kernels  107 us (98%)
  local copies, waits for them, and re-layouts  1.88 us (2%)
    pallas_call x1, Pallas kernels, body(): pl.pallas_call(kernel, out_shape=jax.ShapeDtypeStruct((TOKS, WIDTH), BF16...  107 us

profile of v3, /device:TPU:1, one launch (start us, length us, event | category | flops | bytes accessed | tf_op | source)
XLA Modules:
  0.0 108.5 jit_solution(1117646104418138406)
XLA Ops:
  0.0 106.6 %shard_map.64 = bf16[128,2048]{1,0:T(8,128)(2,1)} custom-call(bf16[128,2048]{1,0:T(8,128)(2,1)} %tok_hbm.1, s32[10,128]{1,0:T(8,128)} %bitcast.2, bf16[10,128]{1,0:T(8,128)(2,1)} %bitcast.3, bf16[4,2048,512]{2,1,0:T(8,128)(2,1)} %wg_hbm.1, bf16[4,2048,512]{2,1,0:T(8,128)(2,1)} %wu_hbm.1, bf16[4,2048,512]{2,1,0:T(8,128)(2,1)} %wd_hbm.1), custom_call_target="tpu_custom_call" | custom-call | tf_op jit(solution)/shard_map/pallas_call | solution.py:410
  106.6 1.9 %copy.8 = bf16[128,2048]{1,0:T(8,128)(2,1)} copy(bf16[128,2048]{1,0:T(8,128)(2,1)} %shard_map.64) | data formatting | bytes 1048576

commit v4 on v3

--- a/solution.py
+++ b/solution.py
@@ -130,22 +130,37 @@
     def rows_of(s):
         return pl.ds(pl.multiple_of(s * CAP, CAP), CAP)
 
+    def several(one, s0, n):
+        at_once = 5 if n % 5 == 0 else 4 if n % 4 == 0 else 3 if n % 3 == 0 else n
+
+        def some(i, carry):
+            for j in range(at_once):
+                one(s0 + i * at_once + j)
+            return carry
+
+        lax.fori_loop(0, n // at_once, some, 0)
+
     def route(b, s0, n):
         for s in range(s0, s0 + n):
             if s > 0:
                 df, dg = ORDER[s]
                 share(b, dg, df).wait_recv()
 
-        def one(s, carry):
+        def weigh(s, carry):
             chosen = g[b, core, s, pl.ds(BODY, META), :].astype(F32)
             gate = g[b, other, s, pl.ds(BODY, META), :].astype(F32)
             for e in range(HELD):
                 mine = (me * HELD + e).astype(F32)
                 ws[s, pl.ds(e, 1), :] = jnp.sum(jnp.where(chosen == mine, gate, 0.0), axis=0, keepdims=True)
-            w = ws[s]
-            rank = jnp.dot((w > 0.0).astype(F32).astype(BF16), before, preferred_element_type=F32)
-            r = jnp.where(w > 0.0, rank, -1.0)
-            ps[s] = r
+            return carry
+
+        lax.fori_loop(s0, s0 + n, weigh, 0)
+        w = ws[pl.ds(s0, n)].reshape(n * 8, TOKS)
+        rank = jnp.dot((w > 0.0).astype(F32).astype(BF16), before, preferred_element_type=F32)
+        ps[pl.ds(s0, n)] = jnp.where(w > 0.0, rank, -1.0).reshape(n, 8, TOKS)
+
+        def one(s):
+            r = ps[s]
             spread = jnp.concatenate(
                 [jnp.where(jnp.broadcast_to(r[e:e + 1], (CAP, TOKS)) == cap_i, 1.0, 0.0) for e in range(HELD)],
                 axis=0).astype(BF16)
@@ -156,9 +171,8 @@
                 picked = jnp.dot(spread, pair, preferred_element_type=F32).astype(BF16)
                 for e in range(HELD):
                     xb[e, rows_of(s), pl.ds(j * 256, 256)] = picked[e * CAP:(e + 1) * CAP]
-            return carry
-
-        lax.fori_loop(s0, s0 + n, one, 0)
+
+        several(one, s0, n)
 
     def expert(e0, n):
         def one(e, carry):
@@ -181,7 +195,7 @@
                       ys.at[b, SLOT[dg, df]], yr.at[b, SLOT[dg, df]], mate)
 
     def combine(b, s0, n):
-        def one(s, carry):
+        def one(s):
             r, w = ps[s], ws[s]
             mix = jnp.concatenate(
                 [jnp.where(jnp.broadcast_to(r[e:e + 1], (CAP, TOKS)) == cap_i,
@@ -193,9 +207,8 @@
                 part = jnp.dot(mix, res, preferred_element_type=F32).astype(BF16)
                 p[b, k, s, pl.ds(c * 128, 128), :] = part[:, :128]
                 p[b, k, s, pl.ds(c * 128 + 128, 128), :] = part[:, 128:]
-            return carry
-
-        lax.fori_loop(s0, s0 + n, one, 0)
+
+        several(one, s0, n)
         if not backs[b]:
             pl.semaphore_wait(free_sem.at[b], 1)
         for s in range(s0, s0 + n):
@@ -216,11 +229,11 @@
 
     def hop(b, phase, df, kind):
         i = home_ids.setdefault((phase, df, kind), len(home_ids))
-        step = 1 if kind in "tp" else -1
-        d = {"t": 2, "b": 2, "p": 1, "m": 3}[kind]
+        step = 1 if kind[0] in "tp" else -1
+        d = {"t": 2, "b": 2, "p": 1, "m": 3}[kind[0]]
         s = SLOT[(df, d) if phase == 1 else (d, 0)]
-        a, n = RET[kind if kind in "tb" else "f"]
-        land = (df * 3 if phase == 1 else 12) + {"t": 0, "b": 0, "p": 1, "m": 2}[kind]
+        a, n = RET[kind[-1]]
+        land = (df * 3 if phase == 1 else 12) + {"t": 0, "b": 0, "p": 1, "m": 2}[kind[0]]
         return remote(p.at[b, 0, s, pl.ds(a, n), :], g.at[b, 0, land, pl.ds(a, n), :],
                       rs.at[b, i], rr.at[b, i], nbr["g" if phase == 1 else "f", step])
 
@@ -229,54 +242,62 @@
         copy.start()
         homes.append(copy)
 
-    def total(b, df, dg, lands):
+    came = set()
+
+    def total(b, df, dg, lands, parts="tb"):
         s = SLOT[df, dg]
-        back(b, dg, df).wait_recv()
-        for part in ("t", "b"):
+        if (b, s) not in came:
+            back(b, dg, df).wait_recv()
+            came.add((b, s))
+        for part in parts:
             a, n = RET[part]
-            terms = [k for k, span in lands if span in ("f", part)]
 
             def add(i, carry):
                 rows = pl.ds(pl.multiple_of(a + i * 128, 128), 128)
                 v = p[b, 0, s, rows, :].astype(F32) + g[b, 1, s, rows, :].astype(F32)
-                for k in terms:
+                for k in lands:
                     v = v + g[b, 0, k, rows, :].astype(F32)
                 p[b, 0, s, rows, :] = v.astype(BF16)
                 return carry
 
             lax.fori_loop(0, n // 128, add, 0)
+
+    def took(b, phase, df, *kinds):
+        for kind in kinds:
+            hop(b, phase, df, kind).wait_recv()
 
     def far(b, df):
         total(b, df, 2, [])
         home(b, 1, df, "t")
         home(b, 1, df, "b")
 
+    def free(b, df):
+        total(b, df, 1, [], "b")
+        home(b, 1, df, "pb")
+        total(b, df, 3, [], "t")
+        home(b, 1, df, "mt")
+
     def near(b, df):
-        hop(b, 1, df, "t").wait_recv()
-        total(b, df, 1, [(df * 3, "t")])
-        home(b, 1, df, "p")
-        hop(b, 1, df, "b").wait_recv()
-        total(b, df, 3, [(df * 3, "b")])
-        home(b, 1, df, "m")
-
-    def column(b, df):
-        hop(b, 1, df, "p").wait_recv()
-        hop(b, 1, df, "m").wait_recv()
-        lands = [(df * 3 + 1, "f"), (df * 3 + 2, "f")]
-        kind = {1: "t", 3: "b"}.get(df)
-        if kind:
-            hop(b, 2, 2, kind).wait_recv()
-            lands.append((12, kind))
+        took(b, 1, df, "t")
+        total(b, df, 1, [df * 3], "t")
+        home(b, 1, df, "pt")
+        took(b, 1, df, "b")
+        total(b, df, 3, [df * 3], "b")
+        home(b, 1, df, "mb")
+
+    def column(b, df, part):
+        took(b, 1, df, "p" + part, "m" + part)
+        lands = [df * 3 + 1, df * 3 + 2]
+        if (df, part) in ((1, "t"), (3, "b")):
+            took(b, 2, 2, part)
+            lands.append(12)
         if df == 0:
-            hop(b, 2, 1, "p").wait_recv()
-            hop(b, 2, 3, "m").wait_recv()
-            lands += [(13, "f"), (14, "f")]
-        total(b, df, 0, lands)
-        if df == 2:
-            home(b, 2, 2, "t")
-            home(b, 2, 2, "b")
-        elif df:
-            home(b, 2, df, "p" if df == 1 else "m")
+            took(b, 2, 1, "p" + part)
+            took(b, 2, 3, "m" + part)
+            lands += [13, 14]
+        total(b, df, 0, lands, part)
+        if df:
+            home(b, 2, df, {1: "p", 2: "", 3: "m"}[df] + part)
 
     def store(src, half, i):
         return [pltpu.make_async_copy(
@@ -286,7 +307,8 @@
     handover = remote(p.at[other, 0, 0], fin, fs, fr, mate)
 
     def finish(b):
-        column(b, 0)
+        column(b, 0, "t")
+        column(b, 0, "b")
 
         @pl.when(core == b)
         def _():
@@ -317,13 +339,13 @@
     arrive(0, 1, 3)
     arrive(0, 3, 1)
     arrive(0, 3, 3)
-    arrive(0, 0, 2)
     route(0, 5, 4)
     arrive(0, 2, 1)
     arrive(0, 2, 3)
     second_ring(1, 0)
     arrive(1, 1, 0)
     arrive(1, 3, 0)
+    arrive(0, 0, 2)
     route(0, 9, 2)
     arrive(0, 1, 2)
     arrive(0, 3, 2)
@@ -344,55 +366,69 @@
     arrive(1, 1, 3)
     expert(2, 1)
     arrive(1, 3, 1)
+    expert(3, 1)
     arrive(1, 3, 3)
-    arrive(1, 0, 2)
-    expert(3, 1)
     combine(0, 11, 5)
     combine(0, 9, 2)
     arrive(1, 2, 1)
+    combine(0, 5, 4)
     arrive(1, 2, 3)
-    combine(0, 5, 4)
+    arrive(1, 0, 2)
     pl.semaphore_wait(ready_sem.at[0], 4)
     far(0, 2)
     far(0, 1)
+    free(0, 2)
     far(0, 3)
     combine(0, 0, 5)
+    free(0, 1)
+    far(0, 0)
+    free(0, 3)
+    free(0, 0)
     arrive(1, 1, 2)
     arrive(1, 3, 2)
     arrive(1, 2, 2)
-    far(0, 0)
     route(1, 0, 5)
+    route(1, 5, 4)
     near(0, 2)
-    route(1, 5, 4)
+    route(1, 9, 7)
+    mate_free(1)
+    ready(1)
+    expert(0, 2)
     near(0, 1)
     near(0, 3)
-    route(1, 9, 7)
-    mate_free(1)
+    expert(2, 1)
     near(0, 0)
-    expert(0, 1)
-    ready(1)
-    expert(1, 1)
-    column(0, 2)
-    expert(2, 2)
-    column(0, 1)
-    column(0, 3)
+    expert(3, 1)
+    column(0, 2, "t")
+    column(0, 2, "b")
     combine(1, 11, 5)
     combine(1, 9, 2)
+    combine(1, 5, 4)
     pl.semaphore_wait(ready_sem.at[1], 4)
     far(1, 2)
     far(1, 1)
+    free(1, 2)
     far(1, 3)
+    column(0, 1, "b")
+    column(0, 3, "t")
+    combine(1, 0, 5)
+    free(1, 1)
+    near(1, 2)
+    column(0, 1, "t")
+    column(0, 3, "b")
     far(1, 0)
-    combine(1, 5, 4)
-    near(1, 2)
-    combine(1, 0, 5)
+    free(1, 3)
     near(1, 1)
     near(1, 3)
-    column(1, 2)
+    column(1, 2, "t")
+    column(1, 2, "b")
+    free(1, 0)
     near(1, 0)
     finish(0)
-    column(1, 1)
-    column(1, 3)
+    column(1, 1, "b")
+    column(1, 3, "t")
+    column(1, 1, "t")
+    column(1, 3, "b")
     finish(1)
     handover.wait_recv()
     rest = store(fin, other, 1)
@@ -427,7 +463,7 @@
             pltpu.VMEM((2, META, TOKS), F32),
             dma((18,)), dma((12,)), dma((2,)), dma((2,)),
             dma((2, 22)), dma((2, 22)), dma((2, 16)), dma((2, 16)), dma((2, 16)), dma((2, 16)),
-            dma((2, 20)), dma((2, 20)), dma, dma, dma((16,)),
+            dma((2, 30)), dma((2, 30)), dma, dma, dma((16,)),
             pltpu.SemaphoreType.REGULAR((2,)), pltpu.SemaphoreType.REGULAR((2,)),
         ],
         compiler_params=pltpu.CompilerParams(

time: 109 us -> 104 us (0.954)
  Pallas kernels: 107 us -> 102 us
    pallas_call x1, Pallas kernels: 107 us -> 102 us  [body(): pl.pallas_call(kernel, out_shape=jax.ShapeDtypeStruct((TOKS, WIDTH), BF16...]
where the time goes in v4:
time: 104 us
  Pallas kernels  102 us (98%)
  local copies, waits for them, and re-layouts  1.88 us (2%)
    pallas_call x1, Pallas kernels, body(): pl.pallas_call(kernel, out_shape=jax.ShapeDtypeStruct((TOKS, WIDTH), BF16...  102 us

profile of v4, /device:TPU:1, one launch (start us, length us, event | category | flops | bytes accessed | tf_op | source)
XLA Modules:
  0.0 104.0 jit_solution(2120332647258210523)
XLA Ops:
  0.0 102.1 %shard_map.64 = bf16[128,2048]{1,0:T(8,128)(2,1)} custom-call(bf16[128,2048]{1,0:T(8,128)(2,1)} %tok_hbm.1, s32[10,128]{1,0:T(8,128)} %bitcast.2, bf16[10,128]{1,0:T(8,128)(2,1)} %bitcast.3, bf16[4,2048,512]{2,1,0:T(8,128)(2,1)} %wg_hbm.1, bf16[4,2048,512]{2,1,0:T(8,128)(2,1)} %wu_hbm.1, bf16[4,2048,512]{2,1,0:T(8,128)(2,1)} %wd_hbm.1), custom_call_target="tpu_custom_call" | custom-call | tf_op jit(solution)/shard_map/pallas_call | solution.py:446
  102.1 1.9 %copy.8 = bf16[128,2048]{1,0:T(8,128)(2,1)} copy(bf16[128,2048]{1,0:T(8,128)(2,1)} %shard_map.64) | data formatting | bytes 1048576

commit v5 on v4

--- a/solution.py
+++ b/solution.py
@@ -20,9 +20,9 @@
 CHIPS = len(ORDER)
 
 
-def kernel(tok_hbm, chosen_hbm, gates_hbm, wg_hbm, wu_hbm, wd_hbm, out_hbm,
+def kernel(tok_hbm, chosen_hbm, gates_hbm, wg_hbm, wu_hbm, wd_hbm, out_ref,
            g, p, wg, wu, wd, xb, ws, ps, fin,
-           ids_v, gates_v, rows_v, own_sem, w_sem, os_, or_, ds, dr, xs, xr, ys, yr, rs, rr, fs, fr, o_sem, free_sem, ready_sem):
+           ids_v, gates_v, rows_v, own_sem, w_sem, os_, or_, es, ds, dr, xs, xr, ys, rs, fs, fr, free_sem, ready_sem):
     me = lax.axis_index("ep")
     core, x, y = me % 2, (me // 2) % SIDE, me // (2 * SIDE)
     other = 1 - core
@@ -52,9 +52,8 @@
     for c in (*routing, *own):
         c.start()
     loads = []
-    for e in range(HELD):
-        for i, (src, dst) in enumerate(((wg_hbm, wg), (wu_hbm, wu), (wd_hbm, wd))):
-            loads.append(pltpu.make_async_copy(src.at[e], dst.at[e], w_sem.at[e * 3 + i]))
+    for i, (src, dst) in enumerate(((wg_hbm, wg), (wu_hbm, wu), (wd_hbm, wd))):
+        loads.append(pltpu.make_async_copy(src, dst, w_sem.at[i]))
     barrier = pltpu.get_barrier_semaphore()
     for n in (*nbr.values(), mate):
         pl.semaphore_signal(barrier, inc=1, device_id={"ep": n}, device_id_type=MESH)
@@ -75,7 +74,7 @@
     for c in halves:
         c.start()
 
-    out_ids, sent, crossed = {}, {0: [], 1: []}, {0: [], 1: []}
+    out_ids, early = {}, {(3, 0, "t"): 0, (1, 0, "b"): 1}
 
     def leg(b, df, dg, part):
         i = out_ids.setdefault((df, dg, part), len(out_ids))
@@ -85,26 +84,27 @@
         s = SLOT[(prev, 0) if dg == 0 else (df, prev)]
         a, n = SPANS[part]
         return remote(g.at[b, 0, s, pl.ds(a, n), :], g.at[b, 0, SLOT[df, dg], pl.ds(a, n), :],
-                      ds.at[b, i], dr.at[b, i], nbr[axis, step])
+                      es.at[early[df, dg, part]] if b == 0 and (df, dg, part) in early else ds.at[b],
+                      dr.at[b, i], nbr[axis, step])
 
     def go(b, *key):
-        copy = leg(b, *key)
-        copy.start()
-        sent[b].append(copy)
+        leg(b, *key).start()
 
     def share(b, df, dg):
         return remote(g.at[b, 0, SLOT[df, dg]], g.at[b, 1, SLOT[dg, df]],
-                      xs.at[b, SLOT[dg, df]], xr.at[b, SLOT[dg, df]], mate)
+                      xs.at[b], xr.at[b, SLOT[dg, df]], mate)
 
     def second_ring(b, df):
         go(b, df, 3, "f")
         go(b, df, 1, "f")
 
-    def first_ring(b):
-        go(b, 3, 0, "t")
-        go(b, 1, 0, "b")
-        go(b, 3, 0, "b")
-        go(b, 1, 0, "t")
+    def first_ring(b, parts=2):
+        if parts != 1:
+            go(b, 3, 0, "t")
+            go(b, 1, 0, "b")
+        if parts != 0:
+            go(b, 3, 0, "b")
+            go(b, 1, 0, "t")
 
     def arrive(b, df, dg):
         if dg == 0:
@@ -118,9 +118,7 @@
                 leg(b, df, dg, part).wait_recv()
             if dg != 2:
                 go(b, df, 2, "t" if dg == 3 else "b")
-        copy = share(b, df, dg)
-        copy.start()
-        crossed[b].append(copy)
+        share(b, df, dg).start()
 
     row_i = lax.broadcasted_iota(jnp.int32, (TOKS, TOKS), 0)
     col_i = lax.broadcasted_iota(jnp.int32, (TOKS, TOKS), 1)
@@ -188,11 +186,14 @@
 
         lax.fori_loop(e0, e0 + n, one, 0)
 
-    backs = {0: [], 1: []}
+    returning = set()
 
     def back(b, df, dg):
-        return remote(p.at[b, 1, SLOT[df, dg]], g.at[b, 1, SLOT[dg, df], pl.ds(0, BODY), :],
-                      ys.at[b, SLOT[dg, df]], yr.at[b, SLOT[dg, df]], mate)
+        return remote(p.at[2, SLOT[df, dg]], g.at[b, 1, SLOT[dg, df], pl.ds(0, BODY), :],
+                      ys.at[b], xr.at[b, SLOT[dg, df]], mate)
+
+    def returned(b):
+        remote(p.at[2], p.at[2], ys.at[b], xr.at[b, 0], mate).wait_send()
 
     def combine(b, s0, n):
         def one(s):
@@ -205,27 +206,27 @@
                 k, c = (j // 4 + core) % 2, (j % 4) * 2
                 res = jnp.concatenate([xb[e, rows_of(s), pl.ds(j * 256, 256)] for e in range(HELD)], axis=0)
                 part = jnp.dot(mix, res, preferred_element_type=F32).astype(BF16)
-                p[b, k, s, pl.ds(c * 128, 128), :] = part[:, :128]
-                p[b, k, s, pl.ds(c * 128 + 128, 128), :] = part[:, 128:]
+                p[b + k * (2 - b), s, pl.ds(c * 128, 128), :] = part[:, :128]
+                p[b + k * (2 - b), s, pl.ds(c * 128 + 128, 128), :] = part[:, 128:]
 
         several(one, s0, n)
-        if not backs[b]:
+        if b not in returning:
             pl.semaphore_wait(free_sem.at[b], 1)
         for s in range(s0, s0 + n):
-            copy = back(b, *ORDER[s])
-            copy.start()
-            backs[b].append(copy)
+            back(b, *ORDER[s]).start()
+        returning.add(b)
 
     def mate_free(b):
         pl.semaphore_signal(free_sem.at[b], inc=1, device_id={"ep": mate}, device_id_type=MESH)
 
     def ready(b):
-        for copy in (*sent[b], *crossed[b]):
-            copy.wait_send()
+        for sem, n in ((ds, 15 if b else 14), (xs, 15)):
+            blocks = g.at[b, 0, pl.ds(0, n)]
+            remote(blocks, blocks, sem.at[b], dr.at[b, 0], mate).wait_send()
         for n in nbr.values():
             pl.semaphore_signal(ready_sem.at[b], inc=1, device_id={"ep": n}, device_id_type=MESH)
 
-    home_ids, homes = {}, []
+    home_ids = {}
 
     def hop(b, phase, df, kind):
         i = home_ids.setdefault((phase, df, kind), len(home_ids))
@@ -234,13 +235,11 @@
         s = SLOT[(df, d) if phase == 1 else (d, 0)]
         a, n = RET[kind[-1]]
         land = (df * 3 if phase == 1 else 12) + {"t": 0, "b": 0, "p": 1, "m": 2}[kind[0]]
-        return remote(p.at[b, 0, s, pl.ds(a, n), :], g.at[b, 0, land, pl.ds(a, n), :],
-                      rs.at[b, i], rr.at[b, i], nbr["g" if phase == 1 else "f", step])
+        return remote(p.at[b, s, pl.ds(a, n), :], g.at[b, 0, land, pl.ds(a, n), :],
+                      rs.at[b], dr.at[b, i], nbr["g" if phase == 1 else "f", step])
 
     def home(*key):
-        copy = hop(*key)
-        copy.start()
-        homes.append(copy)
+        hop(*key).start()
 
     came = set()
 
@@ -254,10 +253,10 @@
 
             def add(i, carry):
                 rows = pl.ds(pl.multiple_of(a + i * 128, 128), 128)
-                v = p[b, 0, s, rows, :].astype(F32) + g[b, 1, s, rows, :].astype(F32)
+                v = p[b, s, rows, :].astype(F32) + g[b, 1, s, rows, :].astype(F32)
                 for k in lands:
                     v = v + g[b, 0, k, rows, :].astype(F32)
-                p[b, 0, s, rows, :] = v.astype(BF16)
+                p[b, s, rows, :] = v.astype(BF16)
                 return carry
 
             lax.fori_loop(0, n // 128, add, 0)
@@ -299,12 +298,11 @@
         if df:
             home(b, 2, df, {1: "p", 2: "", 3: "m"}[df] + part)
 
-    def store(src, half, i):
-        return [pltpu.make_async_copy(
-            src.at[pl.ds(c * 128, 128), :],
-            out_hbm.at[:, pl.ds(pl.multiple_of(half * HALF + c * 128, 128), 128)], o_sem.at[i * 8 + c]) for c in range(8)]
-
-    handover = remote(p.at[other, 0, 0], fin, fs, fr, mate)
+    def store(src, half):
+        for c in range(8):
+            out_ref[:, pl.ds(pl.multiple_of(half * HALF + c * 128, 128), 128)] = src[pl.ds(c * 128, 128), :]
+
+    handover = remote(p.at[other, 0], fin, fs, fr, mate)
 
     def finish(b):
         column(b, 0, "t")
@@ -312,8 +310,7 @@
 
         @pl.when(core == b)
         def _():
-            for c in store(p.at[b, 0, 0], core, 0):
-                c.start()
+            store(p.at[b, 0], core)
 
         @pl.when(core != b)
         def _():
@@ -322,15 +319,15 @@
     for c in halves:
         c.wait_recv()
     first_ring(0)
-    for c in sent[0][:2]:
-        c.wait_send()
-    del sent[0][:2]
+    for key in early:
+        leg(0, *key).wait_send()
     second_ring(0, 0)
+    first_ring(1, 0)
     for c in loads:
         c.start()
     arrive(0, 1, 0)
     arrive(0, 3, 0)
-    first_ring(1)
+    first_ring(1, 1)
     arrive(0, 0, 1)
     arrive(0, 0, 3)
     arrive(0, 2, 0)
@@ -401,6 +398,7 @@
     expert(3, 1)
     column(0, 2, "t")
     column(0, 2, "b")
+    returned(0)
     combine(1, 11, 5)
     combine(1, 9, 2)
     combine(1, 5, 4)
@@ -431,26 +429,24 @@
     column(1, 3, "b")
     finish(1)
     handover.wait_recv()
-    rest = store(fin, other, 1)
-    for c in rest:
-        c.start()
-    for copy in (*backs[0], *backs[1], *homes):
-        copy.wait_send()
+    store(fin, other)
+    returned(1)
+    for b in range(2):
+        sums = p.at[b, pl.ds(0, 15)]
+        remote(sums, sums, rs.at[b], dr.at[b, 0], mate).wait_send()
     handover.wait_send()
-    for c in (*store(p.at[core, 0, 0], core, 0), *rest):
-        c.wait()
 
 
 def body(tokens, experts, gates, w_gate, w_up, w_down):
     dma, any_spec = pltpu.SemaphoreType.DMA, pl.BlockSpec(memory_space=pl.ANY)
     return pl.pallas_call(
         kernel,
-        out_shape=jax.ShapeDtypeStruct((TOKS, WIDTH), BF16),
+        out_shape=pltpu.VMEM((TOKS, WIDTH), BF16),
         in_specs=[any_spec] * 6,
-        out_specs=any_spec,
+        out_specs=pl.BlockSpec(memory_space=pltpu.VMEM),
         scratch_shapes=[
             pltpu.VMEM((2, 2, CHIPS, ROWS, 128), BF16),
-            pltpu.VMEM((2, 2, CHIPS, BODY, 128), BF16),
+            pltpu.VMEM((3, CHIPS, BODY, 128), BF16),
             pltpu.VMEM((HELD, WIDTH, HIDDEN), BF16),
             pltpu.VMEM((HELD, WIDTH, HIDDEN), BF16),
             pltpu.VMEM((HELD, WIDTH, HIDDEN), BF16),
@@ -461,13 +457,12 @@
             pltpu.VMEM((experts.shape[1], TOKS), jnp.int32),
             pltpu.VMEM((gates.shape[1], TOKS), BF16),
             pltpu.VMEM((2, META, TOKS), F32),
-            dma((18,)), dma((12,)), dma((2,)), dma((2,)),
-            dma((2, 22)), dma((2, 22)), dma((2, 16)), dma((2, 16)), dma((2, 16)), dma((2, 16)),
-            dma((2, 30)), dma((2, 30)), dma, dma, dma((16,)),
+            dma((18,)), dma((3,)), dma((2,)), dma((2,)), dma((2,)),
+            dma((2,)), dma((2, 30)), dma((2,)), dma((2, CHIPS)), dma((2,)), dma((2,)), dma, dma,
             pltpu.SemaphoreType.REGULAR((2,)), pltpu.SemaphoreType.REGULAR((2,)),
         ],
         compiler_params=pltpu.CompilerParams(
-            collective_id=0, has_side_effects=True, vmem_limit_bytes=67043328),
+            collective_id=0, has_side_effects=True, vmem_limit_bytes=62000000),
     )(tokens, experts.T, gates.T, w_gate, w_up, w_down)
 
 

time: 104 us -> 99.8 us (0.960)
  Pallas kernels: 102 us -> 98.9 us
  local copies, waits for them, and re-layouts: 1.88 us -> 0.8 us
    pallas_call x1, Pallas kernels: 102 us -> 98.9 us  [body(): pl.pallas_call(kernel, out_shape=pltpu.VMEM((TOKS, WIDTH), BF16), in_spec...]
    unnamed x1, local copies, waits for them, and re-layouts: 1.88 us -> 0.8 us
where the time goes in v5:
time: 99.8 us; the launch traced here: 99.7 us
  Pallas kernels  98.9 us (99%)
    pallas_call x1, Pallas kernels, body(): pl.pallas_call(kernel, out_shape=pltpu.VMEM((TOKS, WIDTH), BF16), in_spec...  98.9 us

profile of v5, /device:TPU:1, one launch (start us, length us, event | category | flops | bytes accessed | tf_op | source)
XLA Modules:
  0.0 99.7 jit_solution(14200159524871914195)
XLA Ops:
  0.0 98.9 %shard_map.64 = bf16[128,2048]{1,0:T(8,128)(2,1)S(1)} custom-call(bf16[128,2048]{1,0:T(8,128)(2,1)} %tok_hbm.1, s32[10,128]{1,0:T(8,128)} %bitcast.2, bf16[10,128]{1,0:T(8,128)(2,1)} %bitcast.3, bf16[4,2048,512]{2,1,0:T(8,128)(2,1)} %wg_hbm.1, bf16[4,2048,512]{2,1,0:T(8,128)(2,1)} %wu_hbm.1, bf16[4,2048,512]{2,1,0:T(8,128)(2,1)} %wd_hbm.1), custom_call_target="tpu_custom_call" | custom-call | tf_op jit(solution)/shard_map/pallas_call | solution.py:442
  98.9 0.8 copy.8

commit v6 on v5

--- a/solution.py
+++ b/solution.py
@@ -42,6 +42,10 @@
         return pltpu.make_async_remote_copy(
             src_ref=src, dst_ref=dst, send_sem=send, recv_sem=recv, device_id={"ep": n}, device_id_type=MESH)
 
+    barrier = pltpu.get_barrier_semaphore()
+    for n in (*nbr.values(), mate):
+        pl.semaphore_signal(barrier, inc=1, device_id={"ep": n}, device_id_type=MESH)
+
     own = []
     for k, half in ((0, core), (1, other)):
         for c in range(8):
@@ -54,9 +58,6 @@
     loads = []
     for i, (src, dst) in enumerate(((wg_hbm, wg), (wu_hbm, wu), (wd_hbm, wd))):
         loads.append(pltpu.make_async_copy(src, dst, w_sem.at[i]))
-    barrier = pltpu.get_barrier_semaphore()
-    for n in (*nbr.values(), mate):
-        pl.semaphore_signal(barrier, inc=1, device_id={"ep": n}, device_id_type=MESH)
     ws[...] = jnp.zeros_like(ws)
     topk = ids_v.shape[0]
     rows_v[0] = jnp.full((META, TOKS), -1.0, F32)
@@ -302,26 +303,30 @@
         for c in range(8):
             out_ref[:, pl.ds(pl.multiple_of(half * HALF + c * 128, 128), 128)] = src[pl.ds(c * 128, 128), :]
 
-    handover = remote(p.at[other, 0], fin, fs, fr, mate)
+    def handover(part):
+        a, n = RET[part]
+        i = "tb".index(part)
+        return remote(p.at[other, 0, pl.ds(a, n), :], fin.at[pl.ds(a, n), :], fs.at[i], fr.at[i], mate)
 
     def finish(b):
-        column(b, 0, "t")
-        column(b, 0, "b")
+        for part in "tb":
+            column(b, 0, part)
+
+            @pl.when(core != b)
+            def _():
+                handover(part).start()
 
         @pl.when(core == b)
         def _():
             store(p.at[b, 0], core)
 
-        @pl.when(core != b)
-        def _():
-            handover.start()
-
-    for c in halves:
-        c.wait_recv()
+    pl.when(core == 1)(halves[0].wait_recv)
     first_ring(0)
     for key in early:
         leg(0, *key).wait_send()
     second_ring(0, 0)
+    pl.when(core == 0)(halves[0].wait_recv)
+    halves[1].wait_recv()
     first_ring(1, 0)
     for c in loads:
         c.start()
@@ -428,13 +433,15 @@
     column(1, 1, "t")
     column(1, 3, "b")
     finish(1)
-    handover.wait_recv()
+    for part in "tb":
+        handover(part).wait_recv()
     store(fin, other)
     returned(1)
     for b in range(2):
         sums = p.at[b, pl.ds(0, 15)]
         remote(sums, sums, rs.at[b], dr.at[b, 0], mate).wait_send()
-    handover.wait_send()
+    for part in "tb":
+        handover(part).wait_send()
 
 
 def body(tokens, experts, gates, w_gate, w_up, w_down):
@@ -458,7 +465,7 @@
             pltpu.VMEM((gates.shape[1], TOKS), BF16),
             pltpu.VMEM((2, META, TOKS), F32),
             dma((18,)), dma((3,)), dma((2,)), dma((2,)), dma((2,)),
-            dma((2,)), dma((2, 30)), dma((2,)), dma((2, CHIPS)), dma((2,)), dma((2,)), dma, dma,
+            dma((2,)), dma((2, 30)), dma((2,)), dma((2, CHIPS)), dma((2,)), dma((2,)), dma((2,)), dma((2,)),
             pltpu.SemaphoreType.REGULAR((2,)), pltpu.SemaphoreType.REGULAR((2,)),
         ],
         compiler_params=pltpu.CompilerParams(

time: 99.8 us -> 99.3 us (level)
  no operation moved by 1% of the time
where the time goes in v6:
time: 99.3 us; the launch traced here: 99.1 us
  Pallas kernels  98.3 us (99%)
    pallas_call x1, Pallas kernels, body(): pl.pallas_call(kernel, out_shape=pltpu.VMEM((TOKS, WIDTH), BF16), in_spec...  98.3 us

profile of v6, /device:TPU:1, one launch (start us, length us, event | category | flops | bytes accessed | tf_op | source)
XLA Modules:
  0.0 99.1 jit_solution(10866229818711659823)
XLA Ops:
  0.0 98.3 %shard_map.64 = bf16[128,2048]{1,0:T(8,128)(2,1)S(1)} custom-call(bf16[128,2048]{1,0:T(8,128)(2,1)} %tok_hbm.1, s32[10,128]{1,0:T(8,128)} %bitcast.2, bf16[10,128]{1,0:T(8,128)(2,1)} %bitcast.3, bf16[4,2048,512]{2,1,0:T(8,128)(2,1)} %wg_hbm.1, bf16[4,2048,512]{2,1,0:T(8,128)(2,1)} %wu_hbm.1, bf16[4,2048,512]{2,1,0:T(8,128)(2,1)} %wd_hbm.1), custom_call_target="tpu_custom_call" | custom-call | tf_op jit(solution)/shard_map/pallas_call | solution.py:449
  98.3 0.8 copy.8
